TPU v7x, 32 devices: a whole 2x2x4 slice. The times are simulated.
32 devices in a mesh: wide: 8 (over z, y), narrow: 4 (over x, core).
Axes of the slice: x: 2, y: 2, z: 4, core: 2. Of those that a mesh axis runs over, the one named last changes fastest.
Arguments:
- entry_factor: bfloat16 [288, 4, 64, 1024], P('wide', 'narrow'), may hold values from -6 to 6
- entry_panel: int32 [288, 4], P('wide', 'narrow'), may hold values from 0 to 1
- entry_target: int32 [288, 4], P('wide', 'narrow'), may hold values from 0 to 7, as said below
- entry_count: int32 [4, 8], P('narrow', 'wide'), may hold values from 1 to 36, 96 in all within a row
- panel_shared: bfloat16 [16, 64, 1024], P('wide', None, 'narrow'), may hold values from -0.1875 to 0.1875
- coupling: float32 [16, 64, 64], P('wide'), may hold values from -0.75 to 0.75
- probes: bfloat16 [32, 64, 1024], P('narrow'), may hold values from -6 to 6
Outputs:
- left_factor: float32 [32, 64, 1024], P('narrow', None, 'wide')
- right_factor: float32 [32, 64, 1024], P('narrow', None, 'wide')
Inputs may be any that keep to these rules, and one draw needn't show every extreme that they name: `entry_panel`: the local panel of an entry of any slot, live or not. `entry_target`: the local target of an entry; every target has at least one live entry. `entry_count`: the live slots of one device; for every owner the counts over the 8 wide indices sum to 96, and some device holds exactly 36.
All inputs are finite; a program needn't handle non-finite values.
Results may differ from a plain program's by a relative error of at most 0.0036.
Values may be sent and summed in bfloat16 or wider, within the bound.
A program may use at most 64 MiB of HBM per device.

v0:
```python
import math

import jax
import jax.numpy as jnp
from jax import lax
from jax.sharding import PartitionSpec as P


def shards(entry_factor, entry_panel, entry_target, entry_count, panel_shared, coupling, probes):
    highest = lax.Precision.HIGHEST
    factors = entry_factor[:, 0]
    slot_count = factors.shape[0]
    rank_dim = factors.shape[1]
    full_width = factors.shape[2]
    panel_count = panel_shared.shape[0]
    target_count = probes.shape[0]
    live_mask = (jnp.arange(slot_count) < entry_count[0, 0]).astype(jnp.float32)
    pick_panel = (entry_panel == jnp.arange(panel_count)[None, :]).astype(jnp.float32) * live_mask[
        :, None
    ]
    pick_target = (entry_target == jnp.arange(target_count)[None, :]).astype(jnp.float32)
    pair_pick = (pick_panel[:, :, None] * pick_target[:, None, :]).reshape(
        slot_count, panel_count * target_count
    )
    gathered = lax.all_gather(panel_shared, "narrow", axis=2, tiled=True)
    projected = jnp.einsum("drb,tkb->dtrk", gathered, probes, preferred_element_type=jnp.float32)
    coefficients = jnp.einsum("dij,dtjk->dtik", coupling, projected, precision=highest).astype(
        jnp.bfloat16
    )
    coeff_table = coefficients.reshape(panel_count * target_count, rank_dim * rank_dim)
    chosen = jnp.dot(
        pair_pick.astype(jnp.bfloat16), coeff_table, preferred_element_type=jnp.float32
    )
    chosen = chosen.astype(jnp.bfloat16).reshape(slot_count, rank_dim, rank_dim)
    contributions = jnp.einsum("eji,ejb->eib", chosen, factors, preferred_element_type=jnp.float32)
    sketch = jnp.einsum("et,eib->tib", pick_target, contributions, precision=highest)
    wide_count = lax.axis_size("wide")
    share_cols = full_width // wide_count
    sketch_sum = lax.psum(sketch, "wide")
    gram_matrix = jnp.einsum("tib,tjb->tij", sketch_sum, sketch_sum, precision=highest)
    lower_factor = jnp.linalg.cholesky(gram_matrix)
    basis = jax.scipy.linalg.solve_triangular(lower_factor, sketch_sum, lower=True)
    basis_round = basis.astype(jnp.bfloat16)
    own_basis = lax.dynamic_slice_in_dim(basis, lax.axis_index("wide") * share_cols, share_cols, 2)
    selected = jnp.einsum(
        "et,tkb->ekb",
        pick_target.astype(jnp.bfloat16),
        basis_round,
        preferred_element_type=jnp.float32,
    )
    selected = selected.astype(jnp.bfloat16)
    back_terms = jnp.einsum("eib,ekb->eik", factors, selected, preferred_element_type=jnp.float32)
    summed = jnp.einsum("ep,eik->pik", pair_pick, back_terms, precision=highest)
    summed = summed.reshape(panel_count, target_count, rank_dim, rank_dim)
    middle_terms = jnp.einsum("dtik,dij->dtkj", summed, coupling, precision=highest)
    partial_rows = jnp.einsum(
        "dtkj,djb->tkb", middle_terms, gathered.astype(jnp.float32), precision=highest
    )
    coeff_part = lax.psum_scatter(partial_rows, "wide", scatter_dimension=2, tiled=True)
    root_width = math.sqrt(full_width)
    return (own_basis * root_width, coeff_part / root_width)


def solution(mesh):
    placed = (
        P("wide", "narrow", None, None),
        P("wide", "narrow"),
        P("wide", "narrow"),
        P("narrow", "wide"),
        P("wide", None, "narrow"),
        P("wide", None, None),
        P("narrow", None, None),
    )
    return jax.shard_map(
        shards,
        mesh=mesh,
        in_specs=placed,
        out_specs=(P("narrow", None, "wide"), P("narrow", None, "wide")),
        check_vma=False,
    )
```

profile of v0, /device:TPU:0, one launch (start us, length us, event | category | flops | bytes accessed | tf_op | source)
XLA Modules:
  0.0 328.4 jit_solution(10725598671400621314)
XLA Ops:
  7.2 0.7 fusion.36
  8.0 7.4 %all_gather.3 = bf16[2,64,1024]{2,1,0:T(8,128)(2,1)S(1)} all-gather(bf16[2,64,256]{2,1,0:T(8,128)(2,1)} %param.11), channel_id=1, replica_groups=mesh['wide'=8,'narrow'=4] {'narrow'}, dimensions={2}, use_global_device_ids=true | all-gather | bytes 327680 | tf_op jit(solution)/shard_map/all_gather | solution.py:25
  15.4 0.5 convolution_bitcast_fusion.1
  16.1 0.6 fusion.18
  18.1 0.6 reshape.99
  18.8 3.8 %fusion.4 = f32[36,64,1024]{2,1,0:T(8,128)S(1)} fusion(bf16[36,64,64]{2,1,0:T(8,128)(2,1)S(1)} %reshape.99, bf16[36,1,64,1024]{3,2,1,0:T(8,128)(2,1)} %param.7), kind=kOutput, calls=%fused_computation.4 | convolution fusion | flops 301989888 | bytes 14450688 | tf_op jit(solution)/shard_map/eji,ejb->eib/dot_general | solution.py:35
  22.6 10.1 %fusion = f32[8,64,1024]{2,0,1:T(8,128)} fusion(f32[36,64,1024]{2,1,0:T(8,128)S(1)} %fusion.4, s32[36]{0:T(128)S(1)} %bitcast.78), kind=kOutput, calls=%fused_computation | convolution fusion | flops 226492704 | bytes 11534480 | tf_op jit(solution)/shard_map/et,eib->tib/dot_general | solution.py:36
  32.8 103.7 %all-reduce.2.cloned.1.call-done = f32[8,64,1024]{2,0,1:T(8,128)} async-done(((f32[8,64,1024]{2,0,1:T(8,128)}), f32[8,64,1024]{2,0,1:T(8,128)}) %all-reduce.2.cloned.1.call-update) | async-done | bytes 2097168 | tf_op jit(solution)/shard_map/psum | solution.py:39
  136.4 6.7 %fusion.9 = f32[8,64,64]{2,1,0:T(8,128)S(1)} fusion(f32[8,64,1024]{2,0,1:T(8,128)} %all-reduce.2.cloned.1.call-done), kind=kOutput, calls=%fused_computation.11 | convolution fusion | flops 402653184 | bytes 2228224 | tf_op jit(solution)/shard_map/tib,tjb->tij/dot_general | solution.py:40
  143.1 0.8 copy.26
  144.0 1.7 fusion.25
  145.7 47.6 %custom-call.8 = f32[8,64,64]{2,1,0:T(8,128)S(1)} custom-call(f32[8,64,64]{2,1,0:T(8,128)} %fusion.25), custom_call_target="Cholesky" | custom-call | tf_op jit(solution)/shard_map/jit(cholesky)/cholesky | solution.py:41
  193.4 0.8 select_bitcast_fusion
  194.3 40.3 %custom-call.9 = f32[8,1,64,64]{2,3,1,0:T(8,128)S(1)} custom-call(f32[8,1,64,64]{3,2,1,0:T(8,128)} %select_bitcast_fusion), custom_call_target="InvertDiagBlocksLowerTriangular" | custom-call | tf_op jit(solution)/shard_map/jit(_solve_triangular)/vmap()/triangular_solve | solution.py:42
  234.5 4.4 %fusion.42 = (bf16[8,64,1024]{2,1,0:T(8,128)(2,1)S(1)}, f32[8,64,1024]{2,1,0:T(8,128)}) fusion(f32[8,64,1024]{2,0,1:T(8,128)S(1)} %copy-done.1, f32[8,1,64,64]{2,3,1,0:T(8,128)S(1)} %custom-call.9), kind=kOutput, calls=%fused_computation.53 | convolution fusion | flops 403177472 | bytes 5373952 | tf_op jit(solution)/shard_map/jit(_solve_triangular)/vmap()/triangular_solve | solution.py:42
  238.9 1.6 convolution_convert_fusion.1
  240.5 5.5 %fusion.11 = f32[36,64,64]{1,2,0:T(8,128)S(1)} fusion(bf16[36,1,64,1024]{3,2,1,0:T(8,128)(2,1)} %param.7, bf16[36,64,1024]{2,0,1:T(8,128)(2,1)S(1)} %convolution_convert_fusion.1), kind=kOutput, calls=%fused_computation.14 | convolution fusion | flops 301989888 | bytes 10027008 | tf_op jit(solution)/shard_map/eib,ekb->eik/dot_general | solution.py:52
  246.0 0.5 copy.31
  246.5 0.8 fusion.16
  247.3 1.8 fusion.21
  249.1 2.3 convolution_bitcast_fusion
  251.5 1.7 dynamic-slice_multiply_fusion
  253.1 66.7 %reduce-scatter.2.cloned.1.call-done = f32[8,64,128]{2,1,0:T(8,128)} async-done(((f32[8,64,1024]{2,1,0:T(8,128)}), f32[8,64,128]{2,1,0:T(8,128)}) %reduce-scatter.2.cloned.1.call-update) | async-done | bytes 262160 | tf_op jit(solution)/shard_map/reduce_scatter | solution.py:59
  319.8 1.7 broadcast_multiply_fusion
  (27 shorter events, 1.3 us)
Async XLA Ops:
  7.2 8.2 %copy-start = (bf16[8,64,1024]{2,1,0:T(8,128)(2,1)S(1)}, bf16[8,64,1024]{2,1,0:T(8,128)(2,1)}, u32[]{:S(2)}) copy-start(bf16[8,64,1024]{2,1,0:T(8,128)(2,1)} %param.13) | copy-start | bytes 3145732
  7.2 8.9 %copy-start.4 = (f32[2,64,64]{2,1,0:T(8,128)S(1)}, f32[2,64,64]{2,1,0:T(8,128)}, u32[]{:S(2)}) copy-start(f32[2,64,64]{2,1,0:T(8,128)} %param.12) | copy-start | bytes 98308
  7.2 10.6 %copy-start.6 = (s32[36,1]{0,1:T(1,128)S(1)}, s32[36,1]{0,1:T(1,128)}, u32[]{:S(2)}) copy-start(s32[36,1]{0,1:T(1,128)} %param.8) | copy-start | bytes 436
  7.2 129.2 %all-reduce.2.cloned.1.call-start = ((), (), s32[]{:S(2)}) async-start(), calls=%async_computation.1 | async-start | bytes 4194304 | tf_op jit(solution)/shard_map/psum | solution.py:39
  15.4 0.7 copy-start.2
  18.8 3.8 %copy-start.5 = (s32[36,1]{0,1:T(1,128)S(1)}, s32[36,1]{0,1:T(1,128)}, u32[]{:S(2)}) copy-start(s32[36,1]{0,1:T(1,128)} %param.9) | copy-start | bytes 436
  32.7 287.2 %reduce-scatter.2.cloned.1.call-start = ((), (), s32[]{:S(2)}) async-start(), calls=%async_computation.2 | async-start | bytes 2359296 | tf_op jit(solution)/shard_map/reduce_scatter | solution.py:59
  136.4 98.1 %copy-start.1 = (f32[8,64,1024]{2,0,1:T(8,128)S(1)}, f32[8,64,1024]{2,0,1:T(8,128)}, u32[]{:S(2)}) copy-start(f32[8,64,1024]{2,0,1:T(8,128)} %all-reduce.2.cloned.1.call-done) | copy-start | bytes 6291460
  246.5 2.6 copy-start.3
Sparse Core Ops, SparseCore 0:
  32.8 103.5 all-reduce.1
  251.6 68.2 reduce-scatter.1
where the time goes:
time: 329 us; the launch traced here: 328 us
  waiting for transfers between devices  170 us (52%)
  other arithmetic  94.6 us (29%)
  matrix products  38.3 us (12%)
  between operations  14.9 us (5%)
  blocking collectives  7.42 us (2%)
    psum x1, waiting for transfers between devices, shards(): sketch_sum = lax.psum(sketch, 'wide')  104 us
    reduce_scatter x1, waiting for transfers between devices, shards(): lax.psum_scatter(partial_rows, 'wide', scatter_dimension=2, tiled=True)  66.7 us
    another operation x4, other arithmetic, shards(): lower_factor = jnp.linalg.cholesky(gram_matrix)  47.8 us
    another operation x3, other arithmetic, shards(): jax.scipy.linalg.solve_triangular(lower_factor, sketch_sum, lower=True)  41.1 us
    dot_general x1, matrix products, shards(): jnp.einsum('et,eib->tib', pick_target, contributions, precision=highest)  10.1 us
    all_gather x1, blocking collectives, shards(): gathered = lax.all_gather(panel_shared, 'narrow', axis=2, tiled=True)  7.42 us
    dot_general x1, matrix products, shards(): jnp.einsum('tib,tjb->tij', sketch_sum, sketch_sum, precision=highest)  6.7 us
  transfers between devices with their start and end apart: 2, of which 2 were waited for; matrix products, arithmetic and copies ran while one was open for 1% of the time, Pallas kernels for 0%

commit v1 on v0

--- a/solution.py
+++ b/solution.py
@@ -36,12 +36,12 @@
     sketch = jnp.einsum("et,eib->tib", pick_target, contributions, precision=highest)
     wide_count = lax.axis_size("wide")
     share_cols = full_width // wide_count
-    sketch_sum = lax.psum(sketch, "wide")
-    gram_matrix = jnp.einsum("tib,tjb->tij", sketch_sum, sketch_sum, precision=highest)
+    sketch_part = lax.psum_scatter(sketch, "wide", scatter_dimension=2, tiled=True)
+    gram_part = jnp.einsum("tib,tjb->tij", sketch_part, sketch_part, precision=highest)
+    gram_matrix = lax.psum(gram_part, "wide")
     lower_factor = jnp.linalg.cholesky(gram_matrix)
-    basis = jax.scipy.linalg.solve_triangular(lower_factor, sketch_sum, lower=True)
-    basis_round = basis.astype(jnp.bfloat16)
-    own_basis = lax.dynamic_slice_in_dim(basis, lax.axis_index("wide") * share_cols, share_cols, 2)
+    own_basis = jax.scipy.linalg.solve_triangular(lower_factor, sketch_part, lower=True)
+    basis_round = lax.all_gather(own_basis.astype(jnp.bfloat16), "wide", axis=2, tiled=True)
     selected = jnp.einsum(
         "et,tkb->ekb",
         pick_target.astype(jnp.bfloat16),

time: 329 us -> 400 us (1.22)
  waiting for transfers between devices: 170 us -> 249 us
  other arithmetic: 94.6 us -> 90.6 us
    reduce_scatter x0 -> x1, waiting for transfers between devices: none -> 70.3 us  [shards(): lax.psum_scatter(sketch, 'wide', scatter_dimension=2, tiled=True)]
    all_gather x0 -> x1, waiting for transfers between devices: none -> 38.7 us  [shards(): lax.all_gather(own_basis.astype(jnp.bfloat16), 'wide', axis=2, tiled=True)]
    psum x1, waiting for transfers between devices: 104 us -> 71.6 us  [shards(): gram_matrix = lax.psum(gram_part, 'wide')]
    dot_general x1, matrix products: 6.7 us -> 2.31 us  [shards(): jnp.einsum('tib,tjb->tij', sketch_part, sketch_part, precision=highest)]
  transfers between devices with their start and end apart: 2 -> 4, of which waited for: 2 -> 4; matrix products, arithmetic and copies ran while one was open for 1% -> 0% of each run, Pallas kernels for 0% -> 0%
where the time goes in v1:
time: 400 us; the launch traced here: 399 us
  waiting for transfers between devices  249 us (62%)
  other arithmetic  90.6 us (23%)
  matrix products  34.9 us (9%)
  between operations  14.6 us (4%)
  blocking collectives  7.42 us (2%)
    psum x1, waiting for transfers between devices, shards(): gram_matrix = lax.psum(gram_part, 'wide')  71.6 us
    reduce_scatter x1, waiting for transfers between devices, shards(): lax.psum_scatter(sketch, 'wide', scatter_dimension=2, tiled=True)  70.3 us
    reduce_scatter x1, waiting for transfers between devices, shards(): lax.psum_scatter(partial_rows, 'wide', scatter_dimension=2, tiled=True)  68 us
    another operation x4, other arithmetic, shards(): lower_factor = jnp.linalg.cholesky(gram_matrix)  47.1 us
    another operation x3, other arithmetic, shards(): jax.scipy.linalg.solve_triangular(lower_factor, sketch_part, lower=True)  39.4 us
    all_gather x1, waiting for transfers between devices, shards(): lax.all_gather(own_basis.astype(jnp.bfloat16), 'wide', axis=2, tiled=True)  38.7 us
    dot_general x1, matrix products, shards(): jnp.einsum('et,eib->tib', pick_target, contributions, precision=highest)  10.1 us
  transfers between devices with their start and end apart: 4, of which 4 were waited for; matrix products, arithmetic and copies ran while one was open for 0% of the time, Pallas kernels for 0%

profile of v1, /device:TPU:0, one launch (start us, length us, event | category | flops | bytes accessed | tf_op | source)
XLA Modules:
  0.0 399.1 jit_solution(11624132694384365650)
XLA Ops:
  7.2 0.7 fusion.36
  8.0 7.4 %all_gather.6 = bf16[2,64,1024]{2,1,0:T(8,128)(2,1)S(1)} all-gather(bf16[2,64,256]{2,1,0:T(8,128)(2,1)} %param.11), channel_id=1, replica_groups=mesh['wide'=8,'narrow'=4] {'narrow'}, dimensions={2}, use_global_device_ids=true | all-gather | bytes 327680 | tf_op jit(solution)/shard_map/all_gather | solution.py:25
  16.1 1.4 fusion.14
  18.7 0.7 compare_select_fusion
  19.6 0.6 reshape.99
  20.3 3.8 fusion.4
  24.1 10.1 %fusion = f32[8,64,1024]{2,0,1:T(8,128)} fusion(f32[36,64,1024]{2,1,0:T(8,128)S(1)} %fusion.4, s32[36]{0:T(128)S(1)} %bitcast.78), kind=kOutput, calls=%fused_computation | convolution fusion | flops 226492704 | bytes 11534480 | tf_op jit(solution)/shard_map/et,eib->tib/dot_general | solution.py:36
  34.3 70.3 %reduce-scatter.3.cloned.1.call-done = f32[8,64,128]{2,0,1:T(8,128)} async-done(((f32[8,64,1024]{2,0,1:T(8,128)}), f32[8,64,128]{2,0,1:T(8,128)}) %reduce-scatter.3.cloned.1.call-update) | async-done | bytes 262160 | tf_op jit(solution)/shard_map/reduce_scatter | solution.py:39
  104.5 2.3 fusion.25
  106.9 71.6 %all-reduce.2.cloned.1.call-done = f32[8,64,64]{1,2,0:T(8,128)} async-done(((f32[8,64,64]{1,2,0:T(8,128)}), f32[8,64,64]{1,2,0:T(8,128)}) %all-reduce.2.cloned.1.call-update) | async-done | bytes 131088 | tf_op jit(solution)/shard_map/psum | solution.py:41
  178.5 1.1 copy.29
  179.6 1.0 fusion.22
  180.6 46.9 %custom-call.8 = f32[8,64,64]{2,1,0:T(8,128)S(1)} custom-call(f32[8,64,64]{2,1,0:T(8,128)S(1)} %fusion.22), custom_call_target="Cholesky" | custom-call | tf_op jit(solution)/shard_map/jit(cholesky)/cholesky | solution.py:42
  227.8 39.3 %custom-call.9 = f32[8,1,64,64]{2,3,1,0:T(8,128)S(1)} custom-call(f32[8,1,64,64]{3,2,1,0:T(8,128)S(1)} %select_bitcast_fusion), custom_call_target="InvertDiagBlocksLowerTriangular" | custom-call | tf_op jit(solution)/shard_map/jit(_solve_triangular)/vmap()/triangular_solve | solution.py:43
  267.1 2.3 fusion.42
  269.5 38.7 %all-gather.2.cloned.1.call-done = bf16[8,64,1024]{2,1,0:T(8,128)(2,1)} async-done(((bf16[8,64,128]{2,1,0:T(8,128)(2,1)}), bf16[8,64,1024]{2,1,0:T(8,128)(2,1)}) %all-gather.2.cloned.1.call-update) | async-done | bytes 1048592 | tf_op jit(solution)/shard_map/all_gather | solution.py:44
  308.2 2.8 convolution_convert_fusion.1
  311.0 5.5 %fusion.7 = f32[36,64,64]{1,2,0:T(8,128)S(1)} fusion(bf16[36,1,64,1024]{3,2,1,0:T(8,128)(2,1)} %param.7, bf16[36,64,1024]{2,0,1:T(8,128)(2,1)S(1)} %convolution_convert_fusion.1), kind=kOutput, calls=%fused_computation.10 | convolution fusion | flops 301989888 | bytes 10027008 | tf_op jit(solution)/shard_map/eib,ekb->eik/dot_general | solution.py:52
  316.4 0.5 copy.34
  316.9 0.8 fusion.12
  317.7 1.8 fusion.17
  319.5 3.3 convolution_bitcast_fusion
  322.9 68.0 %reduce-scatter.5.cloned.1.call-done = f32[8,64,128]{2,1,0:T(8,128)} async-done(((f32[8,64,1024]{2,1,0:T(8,128)}), f32[8,64,128]{2,1,0:T(8,128)}) %reduce-scatter.5.cloned.1.call-update) | async-done | bytes 262160 | tf_op jit(solution)/shard_map/reduce_scatter | solution.py:59
  390.9 1.7 broadcast_multiply_fusion
  (24 shorter events, 2.0 us)
Async XLA Ops:
  7.2 8.2 %copy-start = (bf16[8,64,1024]{2,1,0:T(8,128)(2,1)S(1)}, bf16[8,64,1024]{2,1,0:T(8,128)(2,1)}, u32[]{:S(2)}) copy-start(bf16[8,64,1024]{2,1,0:T(8,128)(2,1)} %param.13) | copy-start | bytes 3145732
  7.2 97.3 %reduce-scatter.3.cloned.1.call-start = ((), (), s32[]{:S(2)}) async-start(), calls=%async_computation.2 | async-start | bytes 2359296 | tf_op jit(solution)/shard_map/reduce_scatter | solution.py:39
  15.4 0.7 copy-start.1
  20.3 3.8 copy-start.2
  34.2 144.3 %all-reduce.2.cloned.1.call-start = ((), (), s32[]{:S(2)}) async-start(), calls=%async_computation.3 | async-start | bytes 524288 | tf_op jit(solution)/shard_map/psum | solution.py:41
  106.9 201.3 %all-gather.2.cloned.1.call-start = ((), (), s32[]{:S(2)}) async-start(), calls=%async_computation.4 | async-start | bytes 1179648 | tf_op jit(solution)/shard_map/all_gather | solution.py:44
  269.4 121.5 %reduce-scatter.5.cloned.1.call-start = ((), (), s32[]{:S(2)}) async-start(), calls=%async_computation.5 | async-start | bytes 2359296 | tf_op jit(solution)/shard_map/reduce_scatter | solution.py:59
Sparse Core Ops, SparseCore 0:
  34.3 70.1 reduce-scatter.2
  108.4 70.0 all-reduce.1
  269.5 38.5 all-gather.1
  323.0 67.8 reduce-scatter.4

commit v2 on v0

--- a/solution.py
+++ b/solution.py
@@ -4,6 +4,20 @@
 import jax.numpy as jnp
 from jax import lax
 from jax.sharding import PartitionSpec as P
+
+
+def wide_reduce(x, count):
+    lead, rows, width = x.shape
+    pieces = x.reshape(lead, rows, count, width // count).transpose(2, 0, 1, 3)
+    pieces = lax.all_to_all(pieces, "wide", 0, 0, tiled=True)
+    return pieces.sum(axis=0)
+
+
+def wide_gather(x, count):
+    lead, rows, width = x.shape
+    copies = jnp.broadcast_to(x[None], (count, lead, rows, width))
+    copies = lax.all_to_all(copies, "wide", 0, 0, tiled=True)
+    return copies.transpose(1, 2, 0, 3).reshape(lead, rows, count * width)
 
 
 def shards(entry_factor, entry_panel, entry_target, entry_count, panel_shared, coupling, probes):
@@ -36,7 +50,7 @@
     sketch = jnp.einsum("et,eib->tib", pick_target, contributions, precision=highest)
     wide_count = lax.axis_size("wide")
     share_cols = full_width // wide_count
-    sketch_sum = lax.psum(sketch, "wide")
+    sketch_sum = wide_gather(wide_reduce(sketch, wide_count), wide_count)
     gram_matrix = jnp.einsum("tib,tjb->tij", sketch_sum, sketch_sum, precision=highest)
     lower_factor = jnp.linalg.cholesky(gram_matrix)
     basis = jax.scipy.linalg.solve_triangular(lower_factor, sketch_sum, lower=True)
@@ -56,7 +70,7 @@
     partial_rows = jnp.einsum(
         "dtkj,djb->tkb", middle_terms, gathered.astype(jnp.float32), precision=highest
     )
-    coeff_part = lax.psum_scatter(partial_rows, "wide", scatter_dimension=2, tiled=True)
+    coeff_part = wide_reduce(partial_rows, wide_count)
     root_width = math.sqrt(full_width)
     return (own_basis * root_width, coeff_part / root_width)
 

time: 329 us -> 296 us (0.90)
  waiting for transfers between devices: 170 us -> 95 us
  blocking collectives: 7.42 us -> 61.8 us
  between operations: 14.9 us -> 1.51 us
  matrix products: 38.3 us -> 30 us
  starting transfers between devices: 0.08 us -> 7.27 us
  local copies, waits for them, and re-layouts: 2.66 us -> 6.03 us
    psum x1 -> x0, waiting for transfers between devices: 104 us -> none  [shards(): sketch_sum = lax.psum(sketch, 'wide')]
    all_to_all x0 -> x2, waiting for transfers between devices: none -> 95 us  [the longest x1 48.3 us: wide_gather(): copies = lax.all_to_all(copies, 'wide', 0, 0, tiled=True)]
    reduce_scatter x1 -> x0, waiting for transfers between devices: 66.7 us -> none  [shards(): lax.psum_scatter(partial_rows, 'wide', scatter_dimension=2, tiled=True)]
    all_to_all x0 -> x1, blocking collectives: none -> 54.4 us  [wide_reduce(): pieces = lax.all_to_all(pieces, 'wide', 0, 0, tiled=True)]
    all_to_all x0 -> x2, starting transfers between devices: none -> 7.27 us  [the longest x1 3.64 us: wide_gather(): copies = lax.all_to_all(copies, 'wide', 0, 0, tiled=True)]
    dot_general x1, matrix products: 6.7 us -> 2.07 us  [shards(): jnp.einsum('tib,tjb->tij', sketch_sum, sketch_sum, precision=highest)]
where the time goes in v2:
time: 296 us; the launch traced here: 295 us
  waiting for transfers between devices  95 us (32%)
  other arithmetic  93.7 us (32%)
  blocking collectives  61.8 us (21%)
  matrix products  30 us (10%)
  starting transfers between devices  7.27 us (2%)
  local copies, waits for them, and re-layouts  6.03 us (2%)
    all_to_all x1, blocking collectives, wide_reduce(): pieces = lax.all_to_all(pieces, 'wide', 0, 0, tiled=True)  54.4 us
    all_to_all x1, waiting for transfers between devices, wide_gather(): copies = lax.all_to_all(copies, 'wide', 0, 0, tiled=True)  48.3 us
    another operation x4, other arithmetic, shards(): lower_factor = jnp.linalg.cholesky(gram_matrix)  47.8 us
    all_to_all x1, waiting for transfers between devices, wide_reduce(): pieces = lax.all_to_all(pieces, 'wide', 0, 0, tiled=True)  46.7 us
    another operation x3, other arithmetic, shards(): jax.scipy.linalg.solve_triangular(lower_factor, sketch_sum, lower=True)  40.9 us
    dot_general x1, matrix products, shards(): jnp.einsum('et,eib->tib', pick_target, contributions, precision=highest)  8.9 us
    all_gather x1, blocking collectives, shards(): gathered = lax.all_gather(panel_shared, 'narrow', axis=2, tiled=True)  7.42 us
  transfers between devices with their start and end apart: 2, of which 2 were waited for; matrix products, arithmetic and copies ran while one was open for 1% of the time, Pallas kernels for 0%

profile of v2, /device:TPU:0, one launch (start us, length us, event | category | flops | bytes accessed | tf_op | source)
XLA Modules:
  0.0 295.4 jit_solution(4871123026989430982)
XLA Ops:
  0.7 0.7 fusion.41
  1.4 7.4 %all_gather.3 = bf16[2,64,1024]{2,1,0:T(8,128)(2,1)S(1)} all-gather(bf16[2,64,256]{2,1,0:T(8,128)(2,1)} %param.11), channel_id=1, replica_groups=mesh['wide'=8,'narrow'=4] {'narrow'}, dimensions={2}, use_global_device_ids=true | all-gather | bytes 327680 | tf_op jit(solution)/shard_map/all_gather | solution.py:39
  12.2 3.8 %fusion.4 = f32[36,64,1024]{2,1,0:T(8,128)S(1)} fusion(bf16[36,64,64]{2,1,0:T(8,128)(2,1)S(1)} %reshape.109, bf16[36,1,64,1024]{3,2,1,0:T(8,128)(2,1)} %param.7), kind=kOutput, calls=%fused_computation.4 | convolution fusion | flops 301989888 | bytes 14450688 | tf_op jit(solution)/shard_map/eji,ejb->eib/dot_general | solution.py:49
  16.0 8.9 %fusion.13 = f32[8,64,8,128]{3,0,2,1:T(8,128)S(1)} fusion(f32[36,64,1024]{2,1,0:T(8,128)S(1)} %fusion.4, s32[36]{0:T(128)S(1)} %bitcast.107), kind=kOutput, calls=%fused_computation.17 | convolution fusion | flops 226492704 | bytes 11534480 | tf_op jit(solution)/shard_map/et,eib->tib/dot_general | solution.py:50
  25.0 54.4 %all_to_all.15 = f32[8,8,64,128]{3,1,2,0:T(8,128)S(1)} all-to-all(f32[8,8,64,128]{3,1,2,0:T(8,128)S(1)} %bitcast.105), channel_id=1, replica_groups=mesh['wide'=8,'narrow'=4] {'wide'}, dimensions={0} | all-to-all | bytes 4194304 | tf_op jit(solution)/shard_map/all_to_all | solution.py:12
  79.6 1.6 broadcast_in_dim.4
  81.2 3.6 %all-to-all-start.1 = ((f32[8,8,64,128]{3,2,1,0:T(8,128)}), f32[8,8,64,128]{3,2,1,0:T(8,128)S(1)}, u32[]{:S(2)}, u32[]{:S(2)}) async-start(f32[8,8,64,128]{3,2,1,0:T(8,128)} %broadcast_in_dim.4), calls=%async_computation.1 | async-start | bytes 4194304 | tf_op jit(solution)/shard_map/all_to_all | solution.py:19
  84.9 48.3 %all-to-all-done.1 = f32[8,8,64,128]{3,2,1,0:T(8,128)S(1)} async-done(((f32[8,8,64,128]{3,2,1,0:T(8,128)}), f32[8,8,64,128]{3,2,1,0:T(8,128)S(1)}, u32[]{:S(2)}, u32[]{:S(2)}) %all-to-all-start.1) | async-done | bytes 2097184 | tf_op jit(solution)/shard_map/all_to_all | solution.py:19
  133.2 2.1 fusion.9
  135.2 0.8 copy.36
  136.1 1.7 fusion.30
  137.7 47.6 %custom-call.8 = f32[8,64,64]{2,1,0:T(8,128)S(1)} custom-call(f32[8,64,64]{2,1,0:T(8,128)} %fusion.30), custom_call_target="Cholesky" | custom-call | tf_op jit(solution)/shard_map/jit(cholesky)/cholesky | solution.py:55
  185.5 0.8 select_bitcast_fusion
  186.3 40.0 %custom-call.9 = f32[8,1,64,64]{2,3,1,0:T(8,128)S(1)} custom-call(f32[8,1,64,64]{3,2,1,0:T(8,128)} %select_bitcast_fusion), custom_call_target="InvertDiagBlocksLowerTriangular" | custom-call | tf_op jit(solution)/shard_map/jit(_solve_triangular)/vmap()/triangular_solve | solution.py:56
  226.4 3.3 %fusion.47 = (bf16[8,64,1024]{2,1,0:T(8,128)(2,1)S(1)}, f32[8,64,1024]{2,1,0:T(8,128)}) fusion(f32[8,1,64,64]{2,3,1,0:T(8,128)S(1)} %custom-call.9, f32[8,8,64,128]{3,2,1,0:T(8,128)S(1)} %all-to-all-done.1), kind=kOutput, calls=%fused_computation.58 | convolution fusion | flops 403177472 | bytes 5373952 | tf_op jit(solution)/shard_map/jit(_solve_triangular)/vmap()/triangular_solve | solution.py:56
  229.7 1.6 convolution_convert_fusion.1
  231.3 5.5 %fusion.16 = f32[36,64,64]{1,2,0:T(8,128)S(1)} fusion(bf16[36,1,64,1024]{3,2,1,0:T(8,128)(2,1)} %param.7, bf16[36,64,1024]{2,0,1:T(8,128)(2,1)S(1)} %convolution_convert_fusion.1), kind=kOutput, calls=%fused_computation.19 | convolution fusion | flops 301989888 | bytes 10027008 | tf_op jit(solution)/shard_map/eib,ekb->eik/dot_general | solution.py:66
  237.2 0.8 fusion.21
  238.0 1.8 fusion.26
  239.9 1.0 convolution_bitcast_fusion
  240.9 1.6 copy.76
  242.5 3.6 %all-to-all-start.2 = ((f32[8,8,64,128]{3,2,1,0:T(8,128)}), f32[8,8,64,128]{3,2,1,0:T(8,128)S(1)}, u32[]{:S(2)}, u32[]{:S(2)}) async-start(f32[8,8,64,128]{3,2,1,0:T(8,128)} %bitcast.104), calls=%async_computation.2 | async-start | bytes 4194304 | tf_op jit(solution)/shard_map/all_to_all | solution.py:12
  246.1 1.7 dynamic-slice_multiply_fusion
  247.8 46.7 %all-to-all-done.2 = f32[8,8,64,128]{3,2,1,0:T(8,128)S(1)} async-done(((f32[8,8,64,128]{3,2,1,0:T(8,128)}), f32[8,8,64,128]{3,2,1,0:T(8,128)S(1)}, u32[]{:S(2)}, u32[]{:S(2)}) %all-to-all-start.2) | async-done | bytes 2097184 | tf_op jit(solution)/shard_map/all_to_all | solution.py:12
  (30 shorter events, 4.5 us)
Async XLA Ops:
  0.6 8.2 %copy-start = (bf16[8,64,1024]{2,1,0:T(8,128)(2,1)S(1)}, bf16[8,64,1024]{2,1,0:T(8,128)(2,1)}, u32[]{:S(2)}) copy-start(bf16[8,64,1024]{2,1,0:T(8,128)(2,1)} %param.13) | copy-start | bytes 3145732
  0.6 8.9 %copy-start.3 = (f32[2,64,64]{2,1,0:T(8,128)S(1)}, f32[2,64,64]{2,1,0:T(8,128)}, u32[]{:S(2)}) copy-start(f32[2,64,64]{2,1,0:T(8,128)} %param.12) | copy-start | bytes 98308
  0.7 10.6 %copy-start.5 = (s32[36,1]{0,1:T(1,128)S(1)}, s32[36,1]{0,1:T(1,128)}, u32[]{:S(2)}) copy-start(s32[36,1]{0,1:T(1,128)} %param.8) | copy-start | bytes 436
  8.8 0.7 copy-start.1
  12.2 3.8 %copy-start.4 = (s32[36,1]{0,1:T(1,128)S(1)}, s32[36,1]{0,1:T(1,128)}, u32[]{:S(2)}) copy-start(s32[36,1]{0,1:T(1,128)} %param.9) | copy-start | bytes 436
  81.2 52.0 %all-to-all-start.1 = ((f32[8,8,64,128]{3,2,1,0:T(8,128)}), f32[8,8,64,128]{3,2,1,0:T(8,128)S(1)}, u32[]{:S(2)}, u32[]{:S(2)}) async-start(f32[8,8,64,128]{3,2,1,0:T(8,128)} %broadcast_in_dim.4), calls=%async_computation.1 | async-start | bytes 4194304 | tf_op jit(solution)/shard_map/all_to_all | solution.py:19
  237.2 2.6 copy-start.2
  242.5 52.1 %all-to-all-start.2 = ((f32[8,8,64,128]{3,2,1,0:T(8,128)}), f32[8,8,64,128]{3,2,1,0:T(8,128)S(1)}, u32[]{:S(2)}, u32[]{:S(2)}) async-start(f32[8,8,64,128]{3,2,1,0:T(8,128)} %bitcast.104), calls=%async_computation.2 | async-start | bytes 4194304 | tf_op jit(solution)/shard_map/all_to_all | solution.py:12

commit v3 on v2

--- a/solution.py
+++ b/solution.py
@@ -18,6 +18,22 @@
     copies = jnp.broadcast_to(x[None], (count, lead, rows, width))
     copies = lax.all_to_all(copies, "wide", 0, 0, tiled=True)
     return copies.transpose(1, 2, 0, 3).reshape(lead, rows, count * width)
+
+
+def lower_inverse(lower):
+    highest = lax.Precision.HIGHEST
+    size = lower.shape[-1]
+    eye = jnp.eye(size, dtype=lower.dtype)
+    diag = jnp.diagonal(lower, axis1=-2, axis2=-1)
+    strict = eye - lower / diag[..., :, None]
+    unit_inverse = eye + strict
+    power = strict
+    for _ in range(max(size - 1, 1).bit_length() - 1):
+        power = jnp.einsum("tij,tjk->tik", power, power, precision=highest)
+        unit_inverse = unit_inverse + jnp.einsum(
+            "tij,tjk->tik", unit_inverse, power, precision=highest
+        )
+    return unit_inverse / diag[..., None, :]
 
 
 def shards(entry_factor, entry_panel, entry_target, entry_count, panel_shared, coupling, probes):
@@ -53,7 +69,9 @@
     sketch_sum = wide_gather(wide_reduce(sketch, wide_count), wide_count)
     gram_matrix = jnp.einsum("tib,tjb->tij", sketch_sum, sketch_sum, precision=highest)
     lower_factor = jnp.linalg.cholesky(gram_matrix)
-    basis = jax.scipy.linalg.solve_triangular(lower_factor, sketch_sum, lower=True)
+    basis = jnp.einsum(
+        "tij,tjb->tib", lower_inverse(lower_factor), sketch_sum, precision=highest
+    )
     basis_round = basis.astype(jnp.bfloat16)
     own_basis = lax.dynamic_slice_in_dim(basis, lax.axis_index("wide") * share_cols, share_cols, 2)
     selected = jnp.einsum(

time: 296 us -> 262 us (0.89)
  other arithmetic: 93.7 us -> 53.9 us
  local copies, waits for them, and re-layouts: 6.03 us -> 10.2 us
    another operation x3 -> x0, other arithmetic: 40.9 us -> none  [shards(): jax.scipy.linalg.solve_triangular(lower_factor, sketch_sum, lower=True)]
    dot_general x0 -> x11, matrix products: none -> 7.36 us  [the longest x1 3.24 us: shards(): jnp.einsum('tij,tjb->tib', lower_inverse(lower_factor), sketch_sum, preci...]
    another operation x1 -> x0, matrix products: 3.29 us -> none  [shards(): jax.scipy.linalg.solve_triangular(lower_factor, sketch_sum, lower=True)]
    another operation x4 -> x3, other arithmetic: 47.8 us -> 47.8 us  [shards(): lower_factor = jnp.linalg.cholesky(gram_matrix)]
where the time goes in v3:
time: 262 us
  waiting for transfers between devices  95 us (36%)
  blocking collectives  61.8 us (24%)
  other arithmetic  53.9 us (21%)
  matrix products  32 us (12%)
  local copies, waits for them, and re-layouts  10.2 us (4%)
  starting transfers between devices  7.27 us (3%)
    all_to_all x1, blocking collectives, wide_reduce(): pieces = lax.all_to_all(pieces, 'wide', 0, 0, tiled=True)  54.4 us
    all_to_all x1, waiting for transfers between devices, wide_gather(): copies = lax.all_to_all(copies, 'wide', 0, 0, tiled=True)  48.3 us
    another operation x3, other arithmetic, shards(): lower_factor = jnp.linalg.cholesky(gram_matrix)  47.8 us
    all_to_all x1, waiting for transfers between devices, wide_reduce(): pieces = lax.all_to_all(pieces, 'wide', 0, 0, tiled=True)  46.7 us
    dot_general x1, matrix products, shards(): jnp.einsum('et,eib->tib', pick_target, contributions, precision=highest)  8.9 us
    all_gather x1, blocking collectives, shards(): gathered = lax.all_gather(panel_shared, 'narrow', axis=2, tiled=True)  7.42 us
  transfers between devices with their start and end apart: 2, of which 2 were waited for; matrix products, arithmetic and copies ran while one was open for 1% of the time, Pallas kernels for 0%

profile of v3, /device:TPU:0, one launch (start us, length us, event | category | flops | bytes accessed | tf_op | source)
XLA Modules:
  0.0 261.8 jit_solution(10561262723809117147)
XLA Ops:
  1.4 7.4 %all_gather.3 = bf16[2,64,1024]{2,1,0:T(8,128)(2,1)S(1)} all-gather(bf16[2,64,256]{2,1,0:T(8,128)(2,1)} %param.11), channel_id=1, replica_groups=mesh['wide'=8,'narrow'=4] {'narrow'}, dimensions={2}, use_global_device_ids=true | all-gather | bytes 327680 | tf_op jit(solution)/shard_map/all_gather | solution.py:55
  12.2 3.8 %fusion.4 = f32[36,64,1024]{2,1,0:T(8,128)S(1)} fusion(bf16[36,64,64]{2,1,0:T(8,128)(2,1)S(1)} %reshape.113, bf16[36,1,64,1024]{3,2,1,0:T(8,128)(2,1)} %param.7), kind=kOutput, calls=%fused_computation.5 | convolution fusion | flops 301989888 | bytes 14450688 | tf_op jit(solution)/shard_map/eji,ejb->eib/dot_general | solution.py:65
  16.0 8.9 %fusion.13 = f32[8,64,8,128]{3,0,2,1:T(8,128)S(1)} fusion(f32[36,64,1024]{2,1,0:T(8,128)S(1)} %fusion.4, s32[36]{0:T(128)S(1)} %bitcast.124), kind=kOutput, calls=%fused_computation.18 | convolution fusion | flops 226492704 | bytes 11534480 | tf_op jit(solution)/shard_map/et,eib->tib/dot_general | solution.py:66
  25.0 54.4 %all_to_all.15 = f32[8,8,64,128]{3,1,2,0:T(8,128)S(1)} all-to-all(f32[8,8,64,128]{3,1,2,0:T(8,128)S(1)} %bitcast.119), channel_id=1, replica_groups=mesh['wide'=8,'narrow'=4] {'wide'}, dimensions={0} | all-to-all | bytes 4194304 | tf_op jit(solution)/shard_map/all_to_all | solution.py:12
  79.6 1.6 broadcast_in_dim.9
  81.2 3.6 %all-to-all-start.1 = ((f32[8,8,64,128]{3,2,1,0:T(8,128)}), f32[8,8,64,128]{3,2,1,0:T(8,128)S(1)}, u32[]{:S(2)}, u32[]{:S(2)}) async-start(f32[8,8,64,128]{3,2,1,0:T(8,128)} %broadcast_in_dim.9), calls=%async_computation.1 | async-start | bytes 4194304 | tf_op jit(solution)/shard_map/all_to_all | solution.py:19
  84.9 48.3 %all-to-all-done.1 = f32[8,8,64,128]{3,2,1,0:T(8,128)S(1)} async-done(((f32[8,8,64,128]{3,2,1,0:T(8,128)}), f32[8,8,64,128]{3,2,1,0:T(8,128)S(1)}, u32[]{:S(2)}, u32[]{:S(2)}) %all-to-all-start.1) | async-done | bytes 2097184 | tf_op jit(solution)/shard_map/all_to_all | solution.py:19
  133.1 2.1 fusion.9
  135.2 0.8 copy.42
  136.0 1.7 fusion.30
  137.7 47.6 %custom-call.4 = f32[8,64,64]{2,1,0:T(8,128)S(1)} custom-call(f32[8,64,64]{2,1,0:T(8,128)} %fusion.30), custom_call_target="Cholesky" | custom-call | tf_op jit(solution)/shard_map/jit(cholesky)/cholesky | solution.py:71
  186.2 1.0 select_select_fusion
  187.2 2.0 copy.43
  189.2 1.5 gather_fusion
  194.9 3.2 %fusion.51 = (bf16[8,64,1024]{2,1,0:T(8,128)(2,1)S(1)}, f32[8,64,1024]{2,1,0:T(8,128)}) fusion(f32[8,64,64]{2,1,0:T(8,128)S(1)} %fusion.24, f32[8,8,64,128]{3,2,1,0:T(8,128)S(1)} %all-to-all-done.1), kind=kOutput, calls=%fused_computation.70 | convolution fusion | flops 403177472 | bytes 5373952 | tf_op jit(solution)/shard_map/tij,tjb->tib/dot_general | solution.py:72
  198.2 1.6 convolution_convert_fusion.1
  199.8 3.1 %fusion.16 = f32[36,64,64]{1,2,0:T(8,128)S(1)} fusion(bf16[36,1,64,1024]{3,2,1,0:T(8,128)(2,1)S(1)} %bitcast.121, bf16[36,64,1024]{2,0,1:T(8,128)(2,1)S(1)} %convolution_convert_fusion.1), kind=kOutput, calls=%fused_computation.20 | convolution fusion | flops 301989888 | bytes 10027008 | tf_op jit(solution)/shard_map/eib,ekb->eik/dot_general | solution.py:84
  203.4 1.0 fusion.21
  204.4 1.8 fusion.27
  206.3 1.0 convolution_bitcast_fusion
  207.3 1.6 copy.83
  208.9 3.6 %all-to-all-start.2 = ((f32[8,8,64,128]{3,2,1,0:T(8,128)}), f32[8,8,64,128]{3,2,1,0:T(8,128)S(1)}, u32[]{:S(2)}, u32[]{:S(2)}) async-start(f32[8,8,64,128]{3,2,1,0:T(8,128)} %bitcast.118), calls=%async_computation.2 | async-start | bytes 4194304 | tf_op jit(solution)/shard_map/all_to_all | solution.py:12
  212.5 1.7 dynamic-slice_multiply_fusion
  214.2 46.7 %all-to-all-done.2 = f32[8,8,64,128]{3,2,1,0:T(8,128)S(1)} async-done(((f32[8,8,64,128]{3,2,1,0:T(8,128)}), f32[8,8,64,128]{3,2,1,0:T(8,128)S(1)}, u32[]{:S(2)}, u32[]{:S(2)}) %all-to-all-start.2) | async-done | bytes 2097184 | tf_op jit(solution)/shard_map/all_to_all | solution.py:12
  (51 shorter events, 10.1 us)
Async XLA Ops:
  0.6 8.2 %copy-start = (bf16[8,64,1024]{2,1,0:T(8,128)(2,1)S(1)}, bf16[8,64,1024]{2,1,0:T(8,128)(2,1)}, u32[]{:S(2)}) copy-start(bf16[8,64,1024]{2,1,0:T(8,128)(2,1)} %param.13) | copy-start | bytes 3145732
  0.6 8.9 %copy-start.4 = (f32[2,64,64]{2,1,0:T(8,128)S(1)}, f32[2,64,64]{2,1,0:T(8,128)}, u32[]{:S(2)}) copy-start(f32[2,64,64]{2,1,0:T(8,128)} %param.12) | copy-start | bytes 98308
  0.7 10.6 %copy-start.6 = (s32[36,1]{0,1:T(1,128)S(1)}, s32[36,1]{0,1:T(1,128)}, u32[]{:S(2)}) copy-start(s32[36,1]{0,1:T(1,128)} %param.8) | copy-start | bytes 436
  8.8 0.7 copy-start.2
  12.2 3.8 %copy-start.5 = (s32[36,1]{0,1:T(1,128)S(1)}, s32[36,1]{0,1:T(1,128)}, u32[]{:S(2)}) copy-start(s32[36,1]{0,1:T(1,128)} %param.9) | copy-start | bytes 436
  81.2 52.0 %all-to-all-start.1 = ((f32[8,8,64,128]{3,2,1,0:T(8,128)}), f32[8,8,64,128]{3,2,1,0:T(8,128)S(1)}, u32[]{:S(2)}, u32[]{:S(2)}) async-start(f32[8,8,64,128]{3,2,1,0:T(8,128)} %broadcast_in_dim.9), calls=%async_computation.1 | async-start | bytes 4194304 | tf_op jit(solution)/shard_map/all_to_all | solution.py:19
  185.3 0.7 copy-start.1
  194.5 5.2 %slice-start = ((s8[4718592]{0:T(1024)(128)(4,1)}), s8[4194304]{0:T(1024)(128)(4,1)S(1)}, s32[]{:S(2)}) async-start(s8[4718592]{0:T(1024)(128)(4,1)} %bitcast.120), calls=%async_computation.3 | async-start | bytes 8388608
  194.9 4.8 %slice-start.1 = ((s8[4718592]{0:T(1024)(128)(4,1)}), s8[524288]{0:T(1024)(128)(4,1)S(1)}, s32[]{:S(2)}) async-start(s8[4718592]{0:T(1024)(128)(4,1)} %bitcast.120), calls=%async_computation.4 | async-start | bytes 1048576
  203.4 2.9 %copy-start.3 = (bf16[2,64,1024]{2,1,0:T(8,128)(2,1)S(1)}, bf16[2,64,1024]{2,1,0:T(8,128)(2,1)}, u32[]{:S(2)}) copy-start(bf16[2,64,1024]{2,1,0:T(8,128)(2,1)} %copy-done.2) | copy-start | bytes 786436
  208.9 52.1 %all-to-all-start.2 = ((f32[8,8,64,128]{3,2,1,0:T(8,128)}), f32[8,8,64,128]{3,2,1,0:T(8,128)S(1)}, u32[]{:S(2)}, u32[]{:S(2)}) async-start(f32[8,8,64,128]{3,2,1,0:T(8,128)} %bitcast.118), calls=%async_computation.2 | async-start | bytes 4194304 | tf_op jit(solution)/shard_map/all_to_all | solution.py:12

commit v4 on v3

--- a/solution.py
+++ b/solution.py
@@ -66,8 +66,11 @@
     sketch = jnp.einsum("et,eib->tib", pick_target, contributions, precision=highest)
     wide_count = lax.axis_size("wide")
     share_cols = full_width // wide_count
-    sketch_sum = wide_gather(wide_reduce(sketch, wide_count), wide_count)
-    gram_matrix = jnp.einsum("tib,tjb->tij", sketch_sum, sketch_sum, precision=highest)
+    sketch_own = wide_reduce(sketch, wide_count)
+    gram_part = jnp.einsum("tib,tjb->tij", sketch_own, sketch_own, precision=highest)
+    gram_copies = jnp.broadcast_to(gram_part[None], (wide_count,) + gram_part.shape)
+    gram_matrix = lax.all_to_all(gram_copies, "wide", 0, 0, tiled=True).sum(axis=0)
+    sketch_sum = wide_gather(sketch_own, wide_count)
     lower_factor = jnp.linalg.cholesky(gram_matrix)
     basis = jnp.einsum(
         "tij,tjb->tib", lower_inverse(lower_factor), sketch_sum, precision=highest

time: 262 us -> 251 us (0.958)
  waiting for transfers between devices: 95 us -> 71.4 us
  starting transfers between devices: 7.27 us -> 13.9 us
    all_to_all x1, waiting for transfers between devices: 48.3 us -> 0.01 us  [wide_gather(): copies = lax.all_to_all(copies, 'wide', 0, 0, tiled=True)]
    all_to_all x0 -> x1, waiting for transfers between devices: none -> 25.8 us  [shards(): lax.all_to_all(gram_copies, 'wide', 0, 0, tiled=True).sum(axis=0)]
    all_to_all x0 -> x1, other arithmetic: none -> 4.51 us  [shards(): lax.all_to_all(gram_copies, 'wide', 0, 0, tiled=True).sum(axis=0)]
    all_to_all x0 -> x1, starting transfers between devices: none -> 3.64 us  [shards(): lax.all_to_all(gram_copies, 'wide', 0, 0, tiled=True).sum(axis=0)]
    unnamed x18 -> x14, local copies, waits for them, and re-layouts: 0.93 us -> 4.46 us
  transfers between devices with their start and end apart: 2 -> 3, of which waited for: 2 -> 2; matrix products, arithmetic and copies ran while one was open for 1% -> 25% of each run, Pallas kernels for 0% -> 0%
where the time goes in v4:
time: 251 us; the launch traced here: 250 us
  waiting for transfers between devices  71.4 us (28%)
  blocking collectives  61.8 us (25%)
  other arithmetic  55.6 us (22%)
  matrix products  34.3 us (14%)
  starting transfers between devices  13.9 us (6%)
  local copies, waits for them, and re-layouts  11.9 us (5%)
    all_to_all x1, blocking collectives, wide_reduce(): pieces = lax.all_to_all(pieces, 'wide', 0, 0, tiled=True)  54.4 us
    another operation x3, other arithmetic, shards(): lower_factor = jnp.linalg.cholesky(gram_matrix)  47.3 us
    all_to_all x1, waiting for transfers between devices, wide_reduce(): pieces = lax.all_to_all(pieces, 'wide', 0, 0, tiled=True)  45.6 us
    all_to_all x1, waiting for transfers between devices, shards(): lax.all_to_all(gram_copies, 'wide', 0, 0, tiled=True).sum(axis=0)  25.8 us
    dot_general x1, matrix products, shards(): jnp.einsum('et,eib->tib', pick_target, contributions, precision=highest)  8.9 us
    all_gather x1, blocking collectives, shards(): gathered = lax.all_gather(panel_shared, 'narrow', axis=2, tiled=True)  7.42 us
    all_to_all x1, starting transfers between devices, wide_reduce(): pieces = lax.all_to_all(pieces, 'wide', 0, 0, tiled=True)  5.91 us
    dot_general x1, matrix products, shards(): jnp.einsum('eib,ekb->eik', factors, selected, preferred_element_type=jnp....  5.48 us
  transfers between devices with their start and end apart: 3, of which 2 were waited for; matrix products, arithmetic and copies ran while one was open for 25% of the time, Pallas kernels for 0%

profile of v4, /device:TPU:0, one launch (start us, length us, event | category | flops | bytes accessed | tf_op | source)
XLA Modules:
  0.0 250.5 jit_solution(6765023599289800090)
XLA Ops:
  0.7 0.7 fusion.42
  1.4 7.4 %all_gather.3 = bf16[2,64,1024]{2,1,0:T(8,128)(2,1)S(1)} all-gather(bf16[2,64,256]{2,1,0:T(8,128)(2,1)} %param.11), channel_id=1, replica_groups=mesh['wide'=8,'narrow'=4] {'narrow'}, dimensions={2}, use_global_device_ids=true | all-gather | bytes 327680 | tf_op jit(solution)/shard_map/all_gather | solution.py:55
  12.2 3.8 %fusion.4 = f32[36,64,1024]{2,1,0:T(8,128)S(1)} fusion(bf16[36,64,64]{2,1,0:T(8,128)(2,1)S(1)} %reshape.114, bf16[36,1,64,1024]{3,2,1,0:T(8,128)(2,1)} %param.7), kind=kOutput, calls=%fused_computation.5 | convolution fusion | flops 301989888 | bytes 14450688 | tf_op jit(solution)/shard_map/eji,ejb->eib/dot_general | solution.py:65
  16.0 8.9 %fusion.10 = f32[8,64,8,128]{3,0,2,1:T(8,128)S(1)} fusion(f32[36,64,1024]{2,1,0:T(8,128)S(1)} %fusion.4, s32[36]{0:T(128)S(1)} %bitcast.117), kind=kOutput, calls=%fused_computation.15 | convolution fusion | flops 226492704 | bytes 11534480 | tf_op jit(solution)/shard_map/et,eib->tib/dot_general | solution.py:66
  25.0 54.4 %all_to_all.20 = f32[8,8,64,128]{3,1,2,0:T(8,128)S(1)} all-to-all(f32[8,8,64,128]{3,1,2,0:T(8,128)S(1)} %bitcast.114), channel_id=1, replica_groups=mesh['wide'=8,'narrow'=4] {'wide'}, dimensions={0} | all-to-all | bytes 4194304 | tf_op jit(solution)/shard_map/all_to_all | solution.py:12
  80.3 2.1 reshape.132
  82.5 3.6 %all-to-all-start.1 = ((f32[8,1,32768]{2,1,0:T(1,128)}), f32[8,1,32768]{2,1,0:T(1,128)S(1)}, u32[]{:S(2)}, u32[]{:S(2)}) async-start(f32[8,1,32768]{2,1,0:T(1,128)} %reshape.132), calls=%async_computation.1 | async-start | bytes 2097152 | tf_op jit(solution)/shard_map/all_to_all | solution.py:72
  86.2 25.8 %all-to-all-done.1 = f32[8,1,32768]{2,1,0:T(1,128)S(1)} async-done(((f32[8,1,32768]{2,1,0:T(1,128)}), f32[8,1,32768]{2,1,0:T(1,128)S(1)}, u32[]{:S(2)}, u32[]{:S(2)}) %all-to-all-start.1) | async-done | bytes 1048608 | tf_op jit(solution)/shard_map/all_to_all | solution.py:72
  112.0 1.6 broadcast_in_dim.12
  113.5 4.3 %all-to-all-start.2 = ((f32[8,8,64,128]{3,2,1,0:T(8,128)}), f32[8,8,64,128]{3,2,1,0:T(8,128)}, u32[]{:S(2)}, u32[]{:S(2)}) async-start(f32[8,8,64,128]{3,2,1,0:T(8,128)} %broadcast_in_dim.12), calls=%async_computation.2 | async-start | bytes 4194304 | tf_op jit(solution)/shard_map/all_to_all | solution.py:19
  118.4 4.5 %reduce.6 = f32[8,32768]{1,0:T(8,128)} reduce(f32[8,1,32768]{2,1,0:T(1,128)S(1)} %all-to-all-done.1, f32[]{:T(128)} %broadcast.125), dimensions={1}, to_apply=%all_to_all.13.reduce_sub_computation | reduce | bytes 2097156 | tf_op jit(solution)/shard_map/all_to_all | solution.py:72
  122.9 2.1 reshape.133
  125.4 47.1 %custom-call.4 = f32[8,64,64]{2,1,0:T(8,128)S(1)} custom-call(f32[8,64,64]{2,1,0:T(8,128)S(1)} %fusion.27), custom_call_target="Cholesky" | custom-call | tf_op jit(solution)/shard_map/jit(cholesky)/cholesky | solution.py:74
  173.4 0.9 gather_fusion
  178.6 4.7 %fusion.50 = (bf16[8,64,1024]{2,1,0:T(8,128)(2,1)S(1)}, f32[8,64,1024]{2,1,0:T(8,128)}) fusion(f32[8,64,64]{2,1,0:T(8,128)S(1)} %fusion.21, f32[8,8,64,128]{3,2,1,0:T(8,128)} %all-to-all-done.2), kind=kOutput, calls=%fused_computation.69 | convolution fusion | flops 403177472 | bytes 5373952 | tf_op jit(solution)/shard_map/tij,tjb->tib/dot_general | solution.py:75
  183.3 1.6 convolution_convert_fusion.1
  184.9 5.5 %fusion.13 = f32[36,64,64]{1,2,0:T(8,128)S(1)} fusion(bf16[36,1,64,1024]{3,2,1,0:T(8,128)(2,1)} %param.7, bf16[36,64,1024]{2,0,1:T(8,128)(2,1)S(1)} %convolution_convert_fusion.1), kind=kOutput, calls=%fused_computation.17 | convolution fusion | flops 301989888 | bytes 10027008 | tf_op jit(solution)/shard_map/eib,ekb->eik/dot_general | solution.py:87
  190.9 1.0 fusion.18
  191.9 1.8 fusion.24
  193.8 1.0 convolution_bitcast_fusion
  194.8 1.6 copy.85
  196.4 5.9 %all-to-all-start.3 = ((f32[8,8,64,128]{3,2,1,0:T(8,128)}), f32[8,8,64,128]{3,2,1,0:T(8,128)S(1)}, u32[]{:S(2)}, u32[]{:S(2)}) async-start(f32[8,8,64,128]{3,2,1,0:T(8,128)} %bitcast.113), calls=%async_computation.3 | async-start | bytes 4194304 | tf_op jit(solution)/shard_map/all_to_all | solution.py:12
  202.4 1.7 dynamic-slice_multiply_fusion
  204.0 45.6 %all-to-all-done.3 = f32[8,8,64,128]{3,2,1,0:T(8,128)S(1)} async-done(((f32[8,8,64,128]{3,2,1,0:T(8,128)}), f32[8,8,64,128]{3,2,1,0:T(8,128)S(1)}, u32[]{:S(2)}, u32[]{:S(2)}) %all-to-all-start.3) | async-done | bytes 2097184 | tf_op jit(solution)/shard_map/all_to_all | solution.py:12
  (52 shorter events, 11.1 us)
Async XLA Ops:
  0.6 8.2 %copy-start = (bf16[8,64,1024]{2,1,0:T(8,128)(2,1)S(1)}, bf16[8,64,1024]{2,1,0:T(8,128)(2,1)}, u32[]{:S(2)}) copy-start(bf16[8,64,1024]{2,1,0:T(8,128)(2,1)} %param.13) | copy-start | bytes 3145732
  0.6 8.9 %copy-start.3 = (f32[2,64,64]{2,1,0:T(8,128)S(1)}, f32[2,64,64]{2,1,0:T(8,128)}, u32[]{:S(2)}) copy-start(f32[2,64,64]{2,1,0:T(8,128)} %param.12) | copy-start | bytes 98308
  0.7 10.6 %copy-start.5 = (s32[36,1]{0,1:T(1,128)S(1)}, s32[36,1]{0,1:T(1,128)}, u32[]{:S(2)}) copy-start(s32[36,1]{0,1:T(1,128)} %param.8) | copy-start | bytes 436
  8.8 0.7 copy-start.1
  12.2 3.8 %copy-start.4 = (s32[36,1]{0,1:T(1,128)S(1)}, s32[36,1]{0,1:T(1,128)}, u32[]{:S(2)}) copy-start(s32[36,1]{0,1:T(1,128)} %param.9) | copy-start | bytes 436
  82.5 29.5 %all-to-all-start.1 = ((f32[8,1,32768]{2,1,0:T(1,128)}), f32[8,1,32768]{2,1,0:T(1,128)S(1)}, u32[]{:S(2)}, u32[]{:S(2)}) async-start(f32[8,1,32768]{2,1,0:T(1,128)} %reshape.132), calls=%async_computation.1 | async-start | bytes 2097152 | tf_op jit(solution)/shard_map/all_to_all | solution.py:72
  113.5 65.1 %all-to-all-start.2 = ((f32[8,8,64,128]{3,2,1,0:T(8,128)}), f32[8,8,64,128]{3,2,1,0:T(8,128)}, u32[]{:S(2)}, u32[]{:S(2)}) async-start(f32[8,8,64,128]{3,2,1,0:T(8,128)} %broadcast_in_dim.12), calls=%async_computation.2 | async-start | bytes 4194304 | tf_op jit(solution)/shard_map/all_to_all | solution.py:19
  190.9 2.9 %copy-start.2 = (bf16[2,64,1024]{2,1,0:T(8,128)(2,1)S(1)}, bf16[2,64,1024]{2,1,0:T(8,128)(2,1)}, u32[]{:S(2)}) copy-start(bf16[2,64,1024]{2,1,0:T(8,128)(2,1)} %copy-done.1) | copy-start | bytes 786436
  196.4 53.1 %all-to-all-start.3 = ((f32[8,8,64,128]{3,2,1,0:T(8,128)}), f32[8,8,64,128]{3,2,1,0:T(8,128)S(1)}, u32[]{:S(2)}, u32[]{:S(2)}) async-start(f32[8,8,64,128]{3,2,1,0:T(8,128)} %bitcast.113), calls=%async_computation.3 | async-start | bytes 4194304 | tf_op jit(solution)/shard_map/all_to_all | solution.py:12

commit v5 on v4

--- a/solution.py
+++ b/solution.py
@@ -88,10 +88,17 @@
     summed = jnp.einsum("ep,eik->pik", pair_pick, back_terms, precision=highest)
     summed = summed.reshape(panel_count, target_count, rank_dim, rank_dim)
     middle_terms = jnp.einsum("dtik,dij->dtkj", summed, coupling, precision=highest)
-    partial_rows = jnp.einsum(
-        "dtkj,djb->tkb", middle_terms, gathered.astype(jnp.float32), precision=highest
-    )
-    coeff_part = wide_reduce(partial_rows, wide_count)
+    half = target_count // 2
+    coeff_halves = []
+    for lo, hi in ((0, half), (half, target_count)):
+        partial_rows = jnp.einsum(
+            "dtkj,djb->tkb",
+            middle_terms[:, lo:hi],
+            gathered.astype(jnp.float32),
+            precision=highest,
+        )
+        coeff_halves.append(wide_reduce(partial_rows, wide_count))
+    coeff_part = jnp.concatenate(coeff_halves, axis=0)
     root_width = math.sqrt(full_width)
     return (own_basis * root_width, coeff_part / root_width)
 

time: 251 us -> 266 us (1.060)
  starting transfers between devices: 13.9 us -> 17.6 us
  local copies, waits for them, and re-layouts: 11.9 us -> 15.4 us
  other arithmetic: 55.6 us -> 58.6 us
    all_to_all x1 -> x2, starting transfers between devices: 5.91 us -> 9.46 us  [wide_reduce(): pieces = lax.all_to_all(pieces, 'wide', 0, 0, tiled=True)]
    all_to_all x1 -> x2, waiting for transfers between devices: 45.6 us -> 47.3 us  [wide_reduce(): pieces = lax.all_to_all(pieces, 'wide', 0, 0, tiled=True)]
  transfers between devices with their start and end apart: 3 -> 4, of which waited for: 2 -> 3; matrix products, arithmetic and copies ran while one was open for 25% -> 26% of each run, Pallas kernels for 0% -> 0%
where the time goes in v5:
time: 266 us; the launch traced here: 265 us
  waiting for transfers between devices  73.1 us (27%)
  blocking collectives  61.8 us (23%)
  other arithmetic  58.6 us (22%)
  matrix products  36.9 us (14%)
  starting transfers between devices  17.6 us (7%)
  local copies, waits for them, and re-layouts  15.4 us (6%)
    all_to_all x1, blocking collectives, wide_reduce(): pieces = lax.all_to_all(pieces, 'wide', 0, 0, tiled=True)  54.4 us
    all_to_all x2, waiting for transfers between devices, wide_reduce(): pieces = lax.all_to_all(pieces, 'wide', 0, 0, tiled=True)  47.3 us
    another operation x3, other arithmetic, shards(): lower_factor = jnp.linalg.cholesky(gram_matrix)  47.3 us
    all_to_all x1, waiting for transfers between devices, shards(): lax.all_to_all(gram_copies, 'wide', 0, 0, tiled=True).sum(axis=0)  25.8 us
    all_to_all x2, starting transfers between devices, wide_reduce(): pieces = lax.all_to_all(pieces, 'wide', 0, 0, tiled=True)  9.46 us
    dot_general x1, matrix products, shards(): jnp.einsum('et,eib->tib', pick_target, contributions, precision=highest)  8.9 us
    all_gather x1, blocking collectives, shards(): gathered = lax.all_gather(panel_shared, 'narrow', axis=2, tiled=True)  7.42 us
    dot_general x1, matrix products, shards(): jnp.einsum('eib,ekb->eik', factors, selected, preferred_element_type=jnp....  6.53 us
  transfers between devices with their start and end apart: 4, of which 3 were waited for; matrix products, arithmetic and copies ran while one was open for 26% of the time, Pallas kernels for 0%

profile of v5, /device:TPU:0, one launch (start us, length us, event | category | flops | bytes accessed | tf_op | source)
XLA Modules:
  0.0 265.1 jit_solution(14758060716650281337)
XLA Ops:
  1.4 7.4 %all_gather.3 = bf16[2,64,1024]{2,1,0:T(8,128)(2,1)S(1)} all-gather(bf16[2,64,256]{2,1,0:T(8,128)(2,1)} %param.11), channel_id=1, replica_groups=mesh['wide'=8,'narrow'=4] {'narrow'}, dimensions={2}, use_global_device_ids=true | all-gather | bytes 327680 | tf_op jit(solution)/shard_map/all_gather | solution.py:55
  12.0 3.8 %fusion.4 = f32[36,64,1024]{2,1,0:T(8,128)S(1)} fusion(bf16[36,64,64]{2,1,0:T(8,128)(2,1)S(1)} %reshape.117, bf16[36,1,64,1024]{3,2,1,0:T(8,128)(2,1)} %param.7), kind=kOutput, calls=%fused_computation.5 | convolution fusion | flops 301989888 | bytes 14450688 | tf_op jit(solution)/shard_map/eji,ejb->eib/dot_general | solution.py:65
  15.8 8.9 %fusion.10 = f32[8,64,8,128]{3,0,2,1:T(8,128)S(1)} fusion(f32[36,64,1024]{2,1,0:T(8,128)S(1)} %fusion.4, s32[36]{0:T(128)S(1)} %bitcast.127), kind=kOutput, calls=%fused_computation.14 | convolution fusion | flops 226492704 | bytes 11534480 | tf_op jit(solution)/shard_map/et,eib->tib/dot_general | solution.py:66
  24.8 54.4 %all_to_all.25 = f32[8,8,64,128]{3,1,2,0:T(8,128)S(1)} all-to-all(f32[8,8,64,128]{3,1,2,0:T(8,128)S(1)} %bitcast.124), channel_id=1, replica_groups=mesh['wide'=8,'narrow'=4] {'wide'}, dimensions={0} | all-to-all | bytes 4194304 | tf_op jit(solution)/shard_map/all_to_all | solution.py:12
  80.0 1.6 fusion.49
  81.9 2.1 reshape.137
  84.0 3.8 %all-to-all-start.1 = ((f32[8,1,32768]{2,1,0:T(1,128)}), f32[8,1,32768]{2,1,0:T(1,128)S(1)}, u32[]{:S(2)}, u32[]{:S(2)}) async-start(f32[8,1,32768]{2,1,0:T(1,128)} %reshape.137), calls=%async_computation.1 | async-start | bytes 2097152 | tf_op jit(solution)/shard_map/all_to_all | solution.py:72
  87.8 25.8 %all-to-all-done.1 = f32[8,1,32768]{2,1,0:T(1,128)S(1)} async-done(((f32[8,1,32768]{2,1,0:T(1,128)}), f32[8,1,32768]{2,1,0:T(1,128)S(1)}, u32[]{:S(2)}, u32[]{:S(2)}) %all-to-all-start.1) | async-done | bytes 1048608 | tf_op jit(solution)/shard_map/all_to_all | solution.py:72
  113.6 1.6 broadcast_in_dim.12
  115.2 4.4 %all-to-all-start.2 = ((f32[8,8,64,128]{3,2,1,0:T(8,128)}), f32[8,8,64,128]{3,2,1,0:T(8,128)}, u32[]{:S(2)}, u32[]{:S(2)}) async-start(f32[8,8,64,128]{3,2,1,0:T(8,128)} %broadcast_in_dim.12), calls=%async_computation.2 | async-start | bytes 4194304 | tf_op jit(solution)/shard_map/all_to_all | solution.py:19
  120.2 4.5 %reduce.6 = f32[8,32768]{1,0:T(8,128)} reduce(f32[8,1,32768]{2,1,0:T(1,128)S(1)} %all-to-all-done.1, f32[]{:T(128)} %broadcast.125), dimensions={1}, to_apply=%all_to_all.16.reduce_sub_computation | reduce | bytes 2097156 | tf_op jit(solution)/shard_map/all_to_all | solution.py:72
  124.7 2.1 reshape.138
  129.8 47.1 %custom-call.4 = f32[8,64,64]{2,1,0:T(8,128)S(1)} custom-call(f32[8,64,64]{2,1,0:T(8,128)S(1)} %fusion.29), custom_call_target="Cholesky" | custom-call | tf_op jit(solution)/shard_map/jit(cholesky)/cholesky | solution.py:74
  177.9 1.6 copy.50
  180.4 1.5 fusion.32
  185.6 4.8 %fusion.51 = (bf16[8,64,1024]{2,1,0:T(8,128)(2,1)S(1)}, f32[8,64,1024]{2,1,0:T(8,128)}) fusion(f32[8,64,64]{2,1,0:T(8,128)S(1)} %fusion.21, f32[8,8,64,128]{3,2,1,0:T(8,128)} %all-to-all-done.2), kind=kOutput, calls=%fused_computation.72 | convolution fusion | flops 403177472 | bytes 5373952 | tf_op jit(solution)/shard_map/tij,tjb->tib/dot_general | solution.py:75
  190.4 1.6 convolution_convert_fusion.1
  192.0 6.5 %fusion.13 = f32[36,64,64]{1,2,0:T(8,128)} fusion(bf16[36,1,64,1024]{3,2,1,0:T(8,128)(2,1)} %param.7, bf16[36,64,1024]{2,0,1:T(8,128)(2,1)S(1)} %convolution_convert_fusion.1), kind=kOutput, calls=%fused_computation.15 | convolution fusion | flops 301989888 | bytes 10027008 | tf_op jit(solution)/shard_map/eib,ekb->eik/dot_general | solution.py:87
  198.5 1.7 copy.57
  204.0 5.9 %all-to-all-start.3 = ((f32[8,4,64,128]{3,2,1,0:T(8,128)}), f32[8,4,64,128]{3,2,1,0:T(8,128)S(1)}, u32[]{:S(2)}, u32[]{:S(2)}) async-start(f32[8,4,64,128]{3,2,1,0:T(8,128)} %bitcast.122), calls=%async_computation.3 | async-start | bytes 2097152 | tf_op jit(solution)/shard_map/all_to_all | solution.py:12
  211.7 23.2 %all-to-all-done.3 = f32[8,4,64,128]{3,2,1,0:T(8,128)S(1)} async-done(((f32[8,4,64,128]{3,2,1,0:T(8,128)}), f32[8,4,64,128]{3,2,1,0:T(8,128)S(1)}, u32[]{:S(2)}, u32[]{:S(2)}) %all-to-all-start.3) | async-done | bytes 1048608 | tf_op jit(solution)/shard_map/all_to_all | solution.py:12
  234.9 3.6 %all-to-all-start.4 = ((f32[8,4,64,128]{3,2,1,0:T(8,128)}), f32[8,4,64,128]{3,2,1,0:T(8,128)S(1)}, u32[]{:S(2)}, u32[]{:S(2)}) async-start(f32[8,4,64,128]{3,2,1,0:T(8,128)} %bitcast.120), calls=%async_computation.4 | async-start | bytes 2097152 | tf_op jit(solution)/shard_map/all_to_all | solution.py:12
  238.5 1.7 dynamic-slice_multiply_fusion
  240.2 24.1 %all-to-all-done.4 = f32[8,4,64,128]{3,2,1,0:T(8,128)S(1)} async-done(((f32[8,4,64,128]{3,2,1,0:T(8,128)}), f32[8,4,64,128]{3,2,1,0:T(8,128)S(1)}, u32[]{:S(2)}, u32[]{:S(2)}) %all-to-all-start.4) | async-done | bytes 1048608 | tf_op jit(solution)/shard_map/all_to_all | solution.py:12
  (57 shorter events, 19.8 us)
Async XLA Ops:
  0.6 8.2 %copy-start = (bf16[8,64,1024]{2,1,0:T(8,128)(2,1)S(1)}, bf16[8,64,1024]{2,1,0:T(8,128)(2,1)}, u32[]{:S(2)}) copy-start(bf16[8,64,1024]{2,1,0:T(8,128)(2,1)} %param.13) | copy-start | bytes 3145732
  0.6 8.7 %copy-start.3 = (f32[2,64,64]{2,1,0:T(8,128)S(1)}, f32[2,64,64]{2,1,0:T(8,128)}, u32[]{:S(2)}) copy-start(f32[2,64,64]{2,1,0:T(8,128)} %param.12) | copy-start | bytes 98308
  0.7 10.4 %copy-start.5 = (s32[36,1]{0,1:T(1,128)S(1)}, s32[36,1]{0,1:T(1,128)}, u32[]{:S(2)}) copy-start(s32[36,1]{0,1:T(1,128)} %param.8) | copy-start | bytes 436
  12.0 3.8 %copy-start.4 = (s32[36,1]{0,1:T(1,128)S(1)}, s32[36,1]{0,1:T(1,128)}, u32[]{:S(2)}) copy-start(s32[36,1]{0,1:T(1,128)} %param.9) | copy-start | bytes 436
  84.0 3.8 %copy-start.1 = (f32[8,64,128]{2,0,1:T(8,128)S(1)}, f32[8,64,128]{2,0,1:T(8,128)}, u32[]{:S(2)}) copy-start(f32[8,64,128]{2,0,1:T(8,128)} %reduce_sum.36) | copy-start | bytes 786436
  84.0 29.6 %all-to-all-start.1 = ((f32[8,1,32768]{2,1,0:T(1,128)}), f32[8,1,32768]{2,1,0:T(1,128)S(1)}, u32[]{:S(2)}, u32[]{:S(2)}) async-start(f32[8,1,32768]{2,1,0:T(1,128)} %reshape.137), calls=%async_computation.1 | async-start | bytes 2097152 | tf_op jit(solution)/shard_map/all_to_all | solution.py:72
  115.2 70.4 %all-to-all-start.2 = ((f32[8,8,64,128]{3,2,1,0:T(8,128)}), f32[8,8,64,128]{3,2,1,0:T(8,128)}, u32[]{:S(2)}, u32[]{:S(2)}) async-start(f32[8,8,64,128]{3,2,1,0:T(8,128)} %broadcast_in_dim.12), calls=%async_computation.2 | async-start | bytes 4194304 | tf_op jit(solution)/shard_map/all_to_all | solution.py:19
  180.3 2.4 copy-start.2
  204.0 30.9 %all-to-all-start.3 = ((f32[8,4,64,128]{3,2,1,0:T(8,128)}), f32[8,4,64,128]{3,2,1,0:T(8,128)S(1)}, u32[]{:S(2)}, u32[]{:S(2)}) async-start(f32[8,4,64,128]{3,2,1,0:T(8,128)} %bitcast.122), calls=%async_computation.3 | async-start | bytes 2097152 | tf_op jit(solution)/shard_map/all_to_all | solution.py:12
  234.9 29.4 %all-to-all-start.4 = ((f32[8,4,64,128]{3,2,1,0:T(8,128)}), f32[8,4,64,128]{3,2,1,0:T(8,128)S(1)}, u32[]{:S(2)}, u32[]{:S(2)}) async-start(f32[8,4,64,128]{3,2,1,0:T(8,128)} %bitcast.120), calls=%async_computation.4 | async-start | bytes 2097152 | tf_op jit(solution)/shard_map/all_to_all | solution.py:12
